TPU v7x, 256 devices: a whole 4x4x8 slice. The times are simulated.
256 devices in a mesh: depth: 16 (over x, y_hi, core), tile: 16 (over y_lo, z).
Axes of the slice: x: 4, y: 4 (y_hi: 2, y_lo: 2; y = y_hi * 2 + y_lo), z: 8, core: 2. Of those that a mesh axis runs over, the one named last changes fastest.
Arguments:
- volume: float32 [32, 2048, 384], P('depth', 'tile'), may hold values from -6 to 6
- point_spread: float32 [32, 255, 255], P('depth'), may hold values from -0.00390625 to 0.00390625
- measured: float32 [2048, 384], P('tile'), may hold values from -6 to 6
Outputs:
- volume_next: float32 [32, 2048, 384], P('depth', 'tile')
- residual: float32 [2048, 384], P('tile')
All inputs are finite; a program needn't handle non-finite values.
Results may differ from a plain program's by a relative error of at most 0.0003.
Values sent between devices are 32-bit elements; how exact they have to be, the bound alone decides.
A program may use at most 64 MiB of HBM per device.

v0:
```python
import functools
import math

import jax
import jax.numpy as jnp
import ml_dtypes
import numpy as np
from jax import lax
from jax.experimental import pallas as pl
from jax.experimental.pallas import tpu as pltpu
from jax.sharding import PartitionSpec as P

step_size = 2.0
threshold = 0.5
f32 = jnp.float32
bf16 = jnp.bfloat16
MESH = pl.DeviceIdType.MESH


def halves(table):
    table = table.astype(np.float32)
    high = table.astype(ml_dtypes.bfloat16)
    low = (table - high.astype(np.float32)).astype(ml_dtypes.bfloat16)
    return np.stack([high, low])


def tables(rows, width, size):
    freq_rows, freq_cols = 3 * rows, width + 128
    half = freq_cols // 2
    reach = (size - 1) // 2
    omega = math.pi * (2 * np.arange(half) + 1) / freq_cols
    across = np.arange(width)[:, None] * omega[None, :]
    col = np.concatenate([np.cos(across), -np.sin(across)], 1)
    back = col.T * (2.0 / (freq_cols * freq_rows))
    across_k = (np.arange(size + 1) - reach)[:, None] * omega[None, :]
    col_k = np.concatenate([np.cos(across_k), -np.sin(across_k)], 1)
    u = np.arange(freq_rows)
    down = 2 * math.pi / freq_rows * (u[:, None] * u[None, :] % freq_rows)
    row = np.concatenate([np.cos(down), np.sin(down)], 0)
    down_k = 2 * math.pi / freq_rows * (u[:, None] * (np.arange(size + 1) - reach)[None, :] % freq_rows)
    row_k = np.concatenate([np.cos(down_k), np.sin(down_k)], 0)
    return [halves(t) for t in (col, back, col_k, row, row_k)]


def split(x):
    high = x.astype(bf16)
    return high, (x - high.astype(f32)).astype(bf16)


def product(a, b):
    left = jnp.concatenate([a[0], a[1], a[0]], axis=1)
    right = jnp.concatenate([b[0], b[0], b[1]], axis=0)
    return jnp.dot(left, right, preferred_element_type=f32)


def turned(a, sign):
    m, n = a.shape[0] // 2, a.shape[1] // 2
    real = a[:m, :n] + sign * a[m:, n:]
    imaginary = a[:m, n:] - sign * a[m:, :n]
    return real, imaginary


def kernel(
    chips,
    strips,
    volume_ref,
    spread_ref,
    measured_ref,
    col_ref,
    back_ref,
    col_k_ref,
    row_ref,
    row_k_ref,
    next_ref,
    residual_ref,
    pad_ref,
    optic_ref,
    mid_ref,
    part_ref,
    pair_ref,
    held_ref,
    beside_ref,
    own_ref,
    piece_ref,
    mine_ref,
    final_ref,
    full_ref,
    pair_sems,
    tile_sems,
    piece_sems,
    final_sems,
    half_sems,
    halo_sems,
    relay_sems,
):
    depth, tile = lax.axis_index("depth"), lax.axis_index("tile")
    chip, core = depth // 2, depth % 2
    partner = chip * 2 + (1 - core)
    above, below = (tile + 1) % strips, (tile + strips - 1) % strips
    others = [(chip + s) % chips * 2 + core for s in range(chips)]
    planes, rows, width = volume_ref.shape
    size = spread_ref.shape[1]
    half_rows = rows // 2
    freq_rows, freq_cols = 3 * rows, width + 128
    half = freq_cols // 2

    barrier = pltpu.get_barrier_semaphore()
    peers = [(partner, tile), (depth, above), (depth, below)] + [(o, tile) for o in others[1:]]
    for d, t in peers:
        pl.semaphore_signal(barrier, inc=1, device_id=(d, t), device_id_type=MESH)

    def remote(src, dst, sems, index, d, t):
        return pltpu.make_async_remote_copy(
            src_ref=src,
            dst_ref=dst,
            send_sem=sems.at[0, index],
            recv_sem=sems.at[1, index],
            device_id=(d, t),
            device_id_type=MESH,
        )

    def pair(ref, *index):
        return ref[(0, *index)], ref[(1, *index)]

    pad_ref[...] = jnp.zeros_like(pad_ref)
    for d in range(planes):
        pad_ref[d, 0:size, 0:size] = spread_ref[d]
    stacked = pad_ref[...].reshape(planes * (size + 1), size + 1)
    optic_cols = product(split(stacked), pair(col_k_ref))
    plane_cols = product(split(volume_ref[...].reshape(planes * rows, width)), pair(col_ref))
    for d in range(planes):
        optic = split(optic_cols[d * (size + 1) : (d + 1) * (size + 1)])
        real, imaginary = turned(product(pair(row_k_ref), optic), 1.0)
        optic_ref[d, 0], optic_ref[d, 1] = real, imaginary
    for d in range(planes):
        plane = split(plane_cols[d * rows : (d + 1) * rows])
        row_part = pair(row_ref, slice(None), slice(0, rows))
        real, imaginary = turned(product(row_part, plane), 1.0)
        optic_real, optic_imaginary = optic_ref[d, 0], optic_ref[d, 1]
        sum_real = optic_real * real - optic_imaginary * imaginary
        sum_imaginary = optic_real * imaginary + optic_imaginary * real
        if d == 0:
            mid_ref[0], mid_ref[1] = sum_real, sum_imaginary
        else:
            mid_ref[0] += sum_real
            mid_ref[1] += sum_imaginary
    total = split(jnp.concatenate([mid_ref[0], mid_ref[1]], axis=1))
    real, imaginary = turned(product(pair(row_ref), total), -1.0)
    mixed = jnp.concatenate([real, imaginary], axis=1)
    part_ref[...] = product(split(mixed), pair(back_ref)).reshape(part_ref.shape)

    pl.semaphore_wait(barrier, len(peers))

    copies = []
    for b in (1, 2, 0):
        copy = remote(part_ref.at[b, 1 - core], pair_ref.at[b], pair_sems, b, partner, tile)
        copy.start()
        copies.append(copy)
    sends = list(copies)
    for b, t in ((1, above), (2, below)):
        copies[b - 1].wait_recv()
        held_ref[b - 1] = part_ref[b, core] + pair_ref[b]
        copy = remote(held_ref.at[b - 1], beside_ref.at[b - 1], tile_sems, b - 1, depth, t)
        copy.start()
        copies.append(copy)
        sends.append(copy)
    copies[2].wait_recv()
    own = part_ref[0, core] + pair_ref[0]
    copies[3].wait_recv()
    own += jnp.where(tile > 0, beside_ref[0], 0.0)
    copies[4].wait_recv()
    own += jnp.where(tile < strips - 1, beside_ref[1], 0.0)
    own_ref[...] = own.reshape(own_ref.shape)

    pieces = []
    for s in range(1, chips):
        copy = remote(own_ref.at[(chip + s) % chips], piece_ref.at[s], piece_sems, s, others[s], tile)
        copy.start()
        pieces.append(copy)
    sends += pieces
    piece = own_ref[chip]
    for s in range(1, chips):
        pieces[s - 1].wait_recv()
        piece += piece_ref[s]
    length = half_rows // chips
    start = pl.multiple_of(core * half_rows + chip * length, length)
    mine_ref[...] = piece - measured_ref[pl.ds(start, length), :]

    finals = []
    for s in range(1, chips):
        copy = remote(mine_ref, final_ref.at[chip], final_sems, s, others[s], tile)
        copy.start()
        finals.append(copy)
    sends += finals
    final_ref[chip] = mine_ref[...]
    for copy in finals:
        copy.wait_recv()
    halves_out = final_ref[...].reshape(half_rows, width)
    full_ref[0, core] = halves_out
    half_copy = remote(full_ref.at[0, core], full_ref.at[0, core], half_sems, 0, partner, tile)
    half_copy.start()
    up = remote(full_ref.at[0, core], full_ref.at[2, core], halo_sems, 0, depth, above)
    up.start()
    down = remote(full_ref.at[0, core], full_ref.at[1, core], halo_sems, 1, depth, below)
    down.start()
    up.wait_recv()
    relay_up = remote(full_ref.at[2, core], full_ref.at[2, core], relay_sems, 0, partner, tile)
    relay_up.start()
    down.wait_recv()
    relay_down = remote(full_ref.at[1, core], full_ref.at[1, core], relay_sems, 1, partner, tile)
    relay_down.start()
    half_copy.wait_recv()
    relay_up.wait_recv()
    relay_down.wait_recv()
    sends += [half_copy, up, down, relay_up, relay_down]

    strip = full_ref[0].reshape(rows, width)
    residual_ref[...] = strip
    after = jnp.where(tile < strips - 1, full_ref[1].reshape(rows, width), 0.0)
    before = jnp.where(tile > 0, full_ref[2].reshape(rows, width), 0.0)
    block = jnp.concatenate([strip, after, before], axis=0)
    block_cols = product(split(block), pair(col_ref))
    real, imaginary = turned(product(pair(row_ref), split(block_cols)), 1.0)
    mid_ref[0], mid_ref[1] = real, imaginary
    for d in range(planes):
        real, imaginary = mid_ref[0], mid_ref[1]
        optic_real, optic_imaginary = optic_ref[d, 0], optic_ref[d, 1]
        grad_real = optic_real * real + optic_imaginary * imaginary
        grad_imaginary = optic_real * imaginary - optic_imaginary * real
        grad = split(jnp.concatenate([grad_real, grad_imaginary], axis=1))
        ends = [jnp.concatenate([row_ref[p, 0:rows], row_ref[p, freq_rows : freq_rows + rows]], axis=0) for p in range(2)]
        real, imaginary = turned(product(ends, grad), -1.0)
        mixed = split(jnp.concatenate([real, imaginary], axis=1))
        gradient = product(mixed, pair(back_ref))
        shifted = volume_ref[d] - step_size * gradient
        next_ref[d] = shifted - jnp.clip(shifted, -threshold, threshold)
    for copy in sends:
        copy.wait_send()


def per_device(volume, point_spread, measured):
    planes, rows, width = volume.shape
    size = point_spread.shape[1]
    chips, strips = lax.axis_size("depth") // 2, lax.axis_size("tile")
    constants = [jnp.asarray(t) for t in tables(rows, width, size)]
    half_rows = rows // 2
    length = half_rows // chips
    freq_rows, half = 3 * rows, (width + 128) // 2
    vmem = pl.BlockSpec(memory_space=pltpu.VMEM)
    dma = pltpu.SemaphoreType.DMA
    return pl.pallas_call(
        functools.partial(kernel, chips, strips),
        out_shape=(
            jax.ShapeDtypeStruct((planes, rows, width), f32),
            jax.ShapeDtypeStruct((rows, width), f32),
        ),
        in_specs=[vmem] * 8,
        out_specs=(vmem, vmem),
        scratch_shapes=[
            pltpu.VMEM((planes, size + 1, size + 1), f32),
            pltpu.VMEM((planes, 2, freq_rows, half), f32),
            pltpu.VMEM((2, freq_rows, half), f32),
            pltpu.VMEM((3, 2, half_rows, width), f32),
            pltpu.VMEM((3, half_rows, width), f32),
            pltpu.VMEM((2, half_rows, width), f32),
            pltpu.VMEM((2, half_rows, width), f32),
            pltpu.VMEM((chips, length, width), f32),
            pltpu.VMEM((chips, length, width), f32),
            pltpu.VMEM((length, width), f32),
            pltpu.VMEM((chips, length, width), f32),
            pltpu.VMEM((3, 2, half_rows, width), f32),
            dma((2, 3)),
            dma((2, 2)),
            dma((2, chips)),
            dma((2, chips)),
            dma((2, 1)),
            dma((2, 2)),
            dma((2, 2)),
        ],
        compiler_params=pltpu.CompilerParams(
            collective_id=0, has_side_effects=True, vmem_limit_bytes=60 * 2**20
        ),
    )(volume, point_spread, measured, *constants)


def solution(mesh):
    placed = (P("depth", "tile", None), P("depth", None, None), P("tile", None))
    return jax.shard_map(
        per_device,
        mesh=mesh,
        in_specs=placed,
        out_specs=(P("depth", "tile", None), P("tile", None)),
        check_vma=False,
    )
```

profile of v0, /device:TPU:1, one launch (start us, length us, event | category | flops | bytes accessed | tf_op | source)
XLA Modules:
  0.0 47.6 jit_solution(3903759632210828441)
XLA Ops:
  0.6 1.9 %copy.10.spread_ref = f32[2,255,255]{2,1,0:T(8,128)} copy(f32[2,255,255]{2,0,1:T(2,128)} %param.9) | data formatting | bytes 1040400 | tf_op args[1]
  2.5 41.7 %shard_map.95 = (f32[2,128,384]{2,1,0:T(8,128)}, f32[128,384]{1,0:T(8,128)}) custom-call(f32[2,128,384]{2,1,0:T(8,128)} %volume_ref.1, f32[2,255,255]{2,1,0:T(8,128)} %copy.10.spread_ref, f32[128,384]{1,0:T(8,128)} %measured_ref.1, bf16[2,384,512]{2,1,0:T(8,128)(2,1)} %constant.10.clone.col_ref, bf16[2,512,384]{2,1,0:T(8,128)(2,1)} %constant.11.clone.back_ref, ...), custom_call_target="tpu_custom_call" | custom-call | tf_op jit(solution)/shard_map/pallas_call | solution.py:251
  44.2 1.8 %copy.13 = f32[2,128,384]{2,1,0:T(8,128)} copy(f32[2,128,384]{2,1,0:T(8,128)} %get-tuple-element.4) | data formatting | bytes 786432
  46.0 1.6 %copy.14 = f32[128,384]{1,0:T(8,128)} copy(f32[128,384]{1,0:T(8,128)} %get-tuple-element.5) | data formatting | bytes 393216
where the time goes:
time: 47.8 us; the launch traced here: 47.6 us
  Pallas kernels  41.7 us (87%)
  local copies, waits for them, and re-layouts  5.25 us (11%)
  between operations  0.64 us (1%)
    pallas_call x1, Pallas kernels, per_device(): pl.pallas_call(functools.partial(kernel, chips, strips), out_shape=(jax.S...  41.7 us
    unnamed x3, local copies, waits for them, and re-layouts  5.25 us

commit v1 on v0

v1 whole, which is shorter than its diff:
```python
import functools
import math

import jax
import jax.numpy as jnp
import ml_dtypes
import numpy as np
from jax import lax
from jax.experimental import pallas as pl
from jax.experimental.pallas import tpu as pltpu
from jax.sharding import PartitionSpec as P

step_size = 2.0
threshold = 0.5
f32 = jnp.float32
bf16 = jnp.bfloat16
MESH = pl.DeviceIdType.MESH


def halves(table):
    table = table.astype(np.float32)
    high = table.astype(ml_dtypes.bfloat16)
    low = (table - high.astype(np.float32)).astype(ml_dtypes.bfloat16)
    return np.stack([high, low])


def tables(rows, width, size):
    freq_rows, freq_cols = 3 * rows, width + 128
    half = freq_cols // 2
    reach = (size - 1) // 2
    omega = math.pi * (2 * np.arange(half) + 1) / freq_cols
    across = np.arange(width)[:, None] * omega[None, :]
    col = np.concatenate([np.cos(across), -np.sin(across)], 1)
    back = col.T * (2.0 / (freq_cols * freq_rows))
    across_k = (np.arange(size + 1) - reach)[:, None] * omega[None, :]
    col_k = np.concatenate([np.cos(across_k), -np.sin(across_k)], 1)
    u = np.arange(freq_rows)
    down = 2 * math.pi / freq_rows * (u[:, None] * u[None, :] % freq_rows)
    row = np.concatenate([np.cos(down), np.sin(down)], 0)
    down_k = 2 * math.pi / freq_rows * (u[:, None] * (np.arange(size + 1) - reach)[None, :] % freq_rows)
    row_k = np.concatenate([np.cos(down_k), np.sin(down_k)], 0)
    return [halves(t) for t in (col, back, col_k, row, row_k)]


def split(x):
    high = x.astype(bf16)
    return high, (x - high.astype(f32)).astype(bf16)


def product(a, b):
    left = jnp.concatenate([a[0], a[1], a[0]], axis=1)
    right = jnp.concatenate([b[0], b[0], b[1]], axis=0)
    return jnp.dot(left, right, preferred_element_type=f32)


def turned(a, sign):
    m, n = a.shape[0] // 2, a.shape[1] // 2
    real = a[:m, :n] + sign * a[m:, n:]
    imaginary = a[:m, n:] - sign * a[m:, :n]
    return real, imaginary


def kernel(
    steps,
    nx,
    strips,
    volume_hbm,
    spread_hbm,
    measured_hbm,
    col_hbm,
    back_hbm,
    col_k_hbm,
    row_hbm,
    row_k_hbm,
    next_ref,
    residual_ref,
    volume_ref,
    spread_ref,
    measured_ref,
    col_ref,
    back_ref,
    col_k_ref,
    row_ref,
    row_k_ref,
    pad_ref,
    optic_ref,
    mid_ref,
    part_ref,
    pair_ref,
    held_ref,
    beside_ref,
    own_ref,
    piece_ref,
    full_ref,
    load_sems,
    pair_sems,
    tile_sems,
    piece_sems,
    final_sems,
    half_sems,
    halo_sems,
    relay_sems,
):
    depth, tile = lax.axis_index("depth"), lax.axis_index("tile")
    chip, core = depth // 2, depth % 2
    x, y = chip // 2, chip % 2
    partner = chip * 2 + (1 - core)
    above, below = (tile + 1) % strips, (tile + strips - 1) % strips
    chips = len(steps)
    targets = [(x + dx) % nx * 2 + (y + dy) % 2 for dx, dy in steps]
    sources = [(x + nx - dx) % nx * 2 + (y + dy) % 2 for dx, dy in steps]
    planes, rows, width = volume_ref.shape
    size = spread_ref.shape[0]
    half_rows = rows // 2
    length = half_rows // chips
    freq_rows, freq_cols = 3 * rows, width + 128
    half = freq_cols // 2

    loads = {}
    order = ("spread", "col_k", "volume", "col", "row_k", "row", "back", "measured")
    refs = {
        "spread": (spread_hbm, spread_ref),
        "col_k": (col_k_hbm, col_k_ref),
        "volume": (volume_hbm, volume_ref),
        "col": (col_hbm, col_ref),
        "row_k": (row_k_hbm, row_k_ref),
        "row": (row_hbm, row_ref),
        "back": (back_hbm, back_ref),
        "measured": (measured_hbm, measured_ref),
    }
    for i, name in enumerate(order):
        loads[name] = pltpu.make_async_copy(*refs[name], load_sems.at[i])
        loads[name].start()

    barrier = pltpu.get_barrier_semaphore()
    peers = [(partner, tile), (depth, above), (depth, below)] + [(t * 2 + core, tile) for t in targets[1:]]
    for d, t in peers:
        pl.semaphore_signal(barrier, inc=1, device_id=(d, t), device_id_type=MESH)

    sends = []

    def remote(src, dst, sems, index, d, t):
        copy = pltpu.make_async_remote_copy(
            src_ref=src,
            dst_ref=dst,
            send_sem=sems.at[(0, *index)],
            recv_sem=sems.at[(1, *index)],
            device_id=(d, t),
            device_id_type=MESH,
        )
        copy.start()
        sends.append(copy)
        return copy

    def pair(ref, *index):
        return ref[(0, *index)], ref[(1, *index)]

    pad_ref[...] = jnp.zeros_like(pad_ref)
    loads["spread"].wait()
    for d in range(planes):
        pad_ref[d, 0:size, 0:size] = spread_ref[:, d, :]
    stacked = pad_ref[...].reshape(planes * (size + 1), size + 1)
    loads["col_k"].wait()
    optic_cols = product(split(stacked), pair(col_k_ref))
    loads["volume"].wait()
    loads["col"].wait()
    plane_cols = product(split(volume_ref[...].reshape(planes * rows, width)), pair(col_ref))
    loads["row_k"].wait()
    for d in range(planes):
        optic = split(optic_cols[d * (size + 1) : (d + 1) * (size + 1)])
        real, imaginary = turned(product(pair(row_k_ref), optic), 1.0)
        optic_ref[d, 0], optic_ref[d, 1] = real, imaginary
    loads["row"].wait()
    for d in range(planes):
        plane = split(plane_cols[d * rows : (d + 1) * rows])
        row_part = pair(row_ref, slice(None), slice(0, rows))
        real, imaginary = turned(product(row_part, plane), 1.0)
        optic_real, optic_imaginary = optic_ref[d, 0], optic_ref[d, 1]
        sum_real = optic_real * real - optic_imaginary * imaginary
        sum_imaginary = optic_real * imaginary + optic_imaginary * real
        if d == 0:
            mid_ref[0], mid_ref[1] = sum_real, sum_imaginary
        else:
            mid_ref[0] += sum_real
            mid_ref[1] += sum_imaginary
    total = split(jnp.concatenate([mid_ref[0], mid_ref[1]], axis=1))

    def strips_of(first, count):
        ends = [
            jnp.concatenate(
                [row_ref[p, k * freq_rows + first * rows : k * freq_rows + (first + count) * rows] for k in range(2)], axis=0
            )
            for p in range(2)
        ]
        real, imaginary = turned(product(ends, total), -1.0)
        mixed = jnp.concatenate([real, imaginary], axis=1)
        part = product(split(mixed), pair(back_ref))
        part_ref[first : first + count] = part.reshape(count, 2, half_rows, width)

    def to_partner(b):
        return remote(part_ref.at[b, 1 - core], pair_ref.at[b], pair_sems, (b,), partner, tile)

    loads["back"].wait()
    strips_of(1, 2)
    pl.semaphore_wait(barrier, len(peers))
    paired = {b: to_partner(b) for b in (1, 2)}
    strips_of(0, 1)
    paired[0] = to_partner(0)

    near = {}
    for b in (1, 2):
        paired[b].wait_recv()
        held_ref[b - 1] = (part_ref[b, core] + pair_ref[b]).reshape(chips, length, width)
    for i in reversed(range(chips)):
        for b, t in ((0, above), (1, below)):
            near[b, i] = remote(held_ref.at[b, targets[i]], beside_ref.at[b, i], tile_sems, (b, i), depth, t)
    paired[0].wait_recv()
    own_ref[...] = (part_ref[0, core] + pair_ref[0]).reshape(chips, length, width)

    pieces = {}
    for i in reversed(range(chips)):
        near[0, i].wait_recv()
        near[1, i].wait_recv()
        value = own_ref[targets[i]]
        value += jnp.where(tile > 0, beside_ref[0, i], 0.0)
        value += jnp.where(tile < strips - 1, beside_ref[1, i], 0.0)
        if i:
            held_ref[2, i] = value
            pieces[i] = remote(held_ref.at[2, i], piece_ref.at[i], piece_sems, (i,), targets[i] * 2 + core, tile)
    loads["measured"].wait()
    start = pl.multiple_of(core * half_rows + chip * length, length)
    value -= measured_ref[pl.ds(start, length), :]
    for i in range(1, chips):
        pieces[i].wait_recv()
        value += piece_ref[i]
    full_ref[0, core, chip] = value

    finals, halos, halved, relayed = {}, {}, {}, {}
    mine = full_ref.at[0, core, chip]
    for i in reversed(range(1, chips)):
        finals[i] = remote(mine, mine, final_sems, (i,), targets[i] * 2 + core, tile)
    for i in range(chips):
        j = sources[i]
        here = full_ref.at[0, core, j]
        if i:
            finals[i].wait_recv()
        halos[0, i] = remote(here, full_ref.at[2, core, j], halo_sems, (0, i), depth, above)
        halos[1, i] = remote(here, full_ref.at[1, core, j], halo_sems, (1, i), depth, below)
        halved[i] = remote(here, here, half_sems, (i,), partner, tile)
    for i in range(chips):
        for b, block in ((0, 2), (1, 1)):
            halos[b, i].wait_recv()
            there = full_ref.at[block, core, sources[i]]
            relayed[b, i] = remote(there, there, relay_sems, (b, i), partner, tile)
    for i in range(chips):
        halved[i].wait_recv()
    strip = full_ref[0].reshape(rows, width)
    residual_ref[...] = strip
    for i in range(chips):
        for b in (0, 1):
            relayed[b, i].wait_recv()
    after = jnp.where(tile < strips - 1, full_ref[1].reshape(rows, width), 0.0)
    before = jnp.where(tile > 0, full_ref[2].reshape(rows, width), 0.0)
    block = jnp.concatenate([strip, after, before], axis=0)
    block_cols = product(split(block), pair(col_ref))
    real, imaginary = turned(product(pair(row_ref), split(block_cols)), 1.0)
    mid_ref[0], mid_ref[1] = real, imaginary
    for d in range(planes):
        real, imaginary = mid_ref[0], mid_ref[1]
        optic_real, optic_imaginary = optic_ref[d, 0], optic_ref[d, 1]
        grad_real = optic_real * real + optic_imaginary * imaginary
        grad_imaginary = optic_real * imaginary - optic_imaginary * real
        grad = split(jnp.concatenate([grad_real, grad_imaginary], axis=1))
        ends = [jnp.concatenate([row_ref[p, 0:rows], row_ref[p, freq_rows : freq_rows + rows]], axis=0) for p in range(2)]
        real, imaginary = turned(product(ends, grad), -1.0)
        mixed = split(jnp.concatenate([real, imaginary], axis=1))
        gradient = product(mixed, pair(back_ref))
        shifted = volume_ref[d] - step_size * gradient
        next_ref[d] = shifted - jnp.clip(shifted, -threshold, threshold)
    for copy in sends:
        copy.wait_send()


def finish(next_ref, residual_ref, next_out, residual_out):
    next_out[...] = next_ref[...]
    residual_out[...] = residual_ref[...]


def per_device(volume, point_spread, measured):
    planes, rows, width = volume.shape
    size = point_spread.shape[1]
    chips, strips = lax.axis_size("depth") // 2, lax.axis_size("tile")
    nx = chips // 2
    steps = sorted(((dx, dy) for dx in range(nx) for dy in range(2)), key=lambda s: (min(s[0], nx - s[0]) + 2 * s[1], s))
    constants = [jnp.asarray(t) for t in tables(rows, width, size)]
    spread = jnp.transpose(point_spread, (1, 0, 2))
    half_rows = rows // 2
    length = half_rows // chips
    freq_rows, half = 3 * rows, (width + 128) // 2
    vmem = pl.BlockSpec(memory_space=pltpu.VMEM)
    dma = pltpu.SemaphoreType.DMA
    inputs = (volume, spread, measured, *constants)
    shapes = (jax.ShapeDtypeStruct((planes, rows, width), f32), jax.ShapeDtypeStruct((rows, width), f32))
    outs = pl.pallas_call(
        functools.partial(kernel, steps, nx, strips),
        out_shape=shapes,
        in_specs=[pl.BlockSpec(memory_space=pltpu.HBM)] * 8,
        out_specs=(vmem, vmem),
        scratch_shapes=[pltpu.VMEM(a.shape, a.dtype) for a in inputs]
        + [
            pltpu.VMEM((planes, size + 1, size + 1), f32),
            pltpu.VMEM((planes, 2, freq_rows, half), f32),
            pltpu.VMEM((2, freq_rows, half), f32),
            pltpu.VMEM((3, 2, half_rows, width), f32),
            pltpu.VMEM((3, half_rows, width), f32),
            pltpu.VMEM((3, chips, length, width), f32),
            pltpu.VMEM((2, chips, length, width), f32),
            pltpu.VMEM((chips, length, width), f32),
            pltpu.VMEM((chips, length, width), f32),
            pltpu.VMEM((3, 2, chips, length, width), f32),
            dma((8,)),
            dma((2, 3)),
            dma((2, 2, chips)),
            dma((2, chips)),
            dma((2, chips)),
            dma((2, chips)),
            dma((2, 2, chips)),
            dma((2, 2, chips)),
        ],
        compiler_params=pltpu.CompilerParams(
            collective_id=0, has_side_effects=True, vmem_limit_bytes=24 * 2**20
        ),
    )(*inputs)
    return pl.pallas_call(
        finish,
        out_shape=shapes,
        in_specs=[vmem, vmem],
        out_specs=(vmem, vmem),
        compiler_params=pltpu.CompilerParams(vmem_limit_bytes=8 * 2**20),
    )(*outs)


def solution(mesh):
    placed = (P("depth", "tile", None), P("depth", None, None), P("tile", None))
    return jax.shard_map(
        per_device,
        mesh=mesh,
        in_specs=placed,
        out_specs=(P("depth", "tile", None), P("tile", None)),
        check_vma=False,
    )
```

time: 47.8 us -> 49 us (1.025)
  local copies, waits for them, and re-layouts: 5.25 us -> 8.67 us
  Pallas kernels: 41.7 us -> 39.2 us
    unnamed x3 -> x16, local copies, waits for them, and re-layouts: 5.25 us -> 8.67 us
    pallas_call x1 -> x2, Pallas kernels: 41.7 us -> 39.2 us  [the longest x1 38.4 us: per_device(): pl.pallas_call(functools.partial(kernel, steps, nx, strips), out_shape=sh...]
where the time goes in v1:
time: 49 us; the launch traced here: 48.6 us
  Pallas kernels  39.2 us (80%)
  local copies, waits for them, and re-layouts  8.67 us (18%)
  between operations  0.65 us (1%)
    pallas_call x1, Pallas kernels, per_device(): pl.pallas_call(functools.partial(kernel, steps, nx, strips), out_shape=sh...  38.4 us
    unnamed x16, local copies, waits for them, and re-layouts  8.67 us

profile of v1, /device:TPU:1, one launch (start us, length us, event | category | flops | bytes accessed | tf_op | source)
XLA Modules:
  0.0 48.6 jit_solution(4119024982214281526)
XLA Ops:
  0.6 0.0 copy-start
  0.6 1.3 %copy-done = bf16[2,768,384]{2,1,0:T(8,128)(2,1)S(1)} copy-done((bf16[2,768,384]{2,1,0:T(8,128)(2,1)S(1)}, bf16[2,768,384]{2,1,0:T(8,128)(2,1)}, u32[]{:S(2)}) %copy-start) | copy-done | bytes 1179672
  1.9 0.0 copy-start.1
  1.9 1.1 %copy-done.1 = bf16[2,768,256]{2,1,0:T(8,128)(2,1)S(1)} copy-done((bf16[2,768,256]{2,1,0:T(8,128)(2,1)S(1)}, bf16[2,768,256]{2,1,0:T(8,128)(2,1)}, u32[]{:S(2)}) %copy-start.1) | copy-done | bytes 786456
  3.0 0.0 copy-start.2
  3.0 1.1 %copy-done.2 = bf16[2,512,384]{2,1,0:T(8,128)(2,1)S(1)} copy-done((bf16[2,512,384]{2,1,0:T(8,128)(2,1)S(1)}, bf16[2,512,384]{2,1,0:T(8,128)(2,1)}, u32[]{:S(2)}) %copy-start.2) | copy-done | bytes 786456
  4.2 0.0 copy-start.3
  4.2 1.1 %copy-done.3 = bf16[2,384,512]{2,1,0:T(8,128)(2,1)S(1)} copy-done((bf16[2,384,512]{2,1,0:T(8,128)(2,1)S(1)}, bf16[2,384,512]{2,1,0:T(8,128)(2,1)}, u32[]{:S(2)}) %copy-start.3) | copy-done | bytes 786456
  5.3 0.0 copy-start.4
  5.3 1.0 %copy-done.4 = bf16[2,256,512]{2,1,0:T(8,128)(2,1)S(1)} copy-done((bf16[2,256,512]{2,1,0:T(8,128)(2,1)S(1)}, bf16[2,256,512]{2,1,0:T(8,128)(2,1)}, u32[]{:S(2)}) %copy-start.4) | copy-done | bytes 524312
  6.3 0.0 copy-start.5
  6.3 1.0 %copy-done.5 = f32[2,255,255]{2,0,1:T(2,128)S(1)} copy-done((f32[2,255,255]{2,0,1:T(2,128)S(1)}, f32[2,255,255]{2,0,1:T(2,128)}, u32[]{:S(2)}) %copy-start.5) | copy-done | bytes 520224
  7.4 0.0 copy-start.6
  7.4 1.0 %copy-done.6 = f32[2,128,384]{2,1,0:T(8,128)S(1)} copy-done((f32[2,128,384]{2,1,0:T(8,128)S(1)}, f32[2,128,384]{2,1,0:T(8,128)}, u32[]{:S(2)}) %copy-start.6) | copy-done | bytes 393240
  8.4 0.0 copy-start.7
  8.4 0.9 %copy-done.7 = f32[128,384]{1,0:T(8,128)S(1)} copy-done((f32[128,384]{1,0:T(8,128)S(1)}, f32[128,384]{1,0:T(8,128)}, u32[]{:S(2)}) %copy-start.7) | copy-done | bytes 196632
  9.3 38.4 %shard_map.95 = (f32[2,128,384]{2,1,0:T(8,128)S(1)}, f32[128,384]{1,0:T(8,128)S(1)}) custom-call(f32[2,128,384]{2,1,0:T(8,128)S(1)} %copy-done.6, f32[255,2,255]{2,1,0:T(2,128)S(1)} %bitcast.1, f32[128,384]{1,0:T(8,128)S(1)} %copy-done.7, bf16[2,384,512]{2,1,0:T(8,128)(2,1)S(1)} %copy-done.3, bf16[2,512,384]{2,1,0:T(8,128)(2,1)S(1)} %copy-done.2, ...), custom_call_target="tpu_custom_call" | custom-call | tf_op jit(solution)/shard_map/pallas_call | solution.py:304
  47.7 0.8 %shard_map.96 = (f32[2,128,384]{2,1,0:T(8,128)}, f32[128,384]{1,0:T(8,128)}) custom-call(f32[2,128,384]{2,1,0:T(8,128)S(1)} %get-tuple-element.4.next_ref, f32[128,384]{1,0:T(8,128)S(1)} %get-tuple-element.5.residual_ref), custom_call_target="tpu_custom_call" | custom-call | tf_op jit(solution)/shard_map/pallas_call | solution.py:334
Async XLA Ops:
  0.6 1.3 %copy-start = (bf16[2,768,384]{2,1,0:T(8,128)(2,1)S(1)}, bf16[2,768,384]{2,1,0:T(8,128)(2,1)}, u32[]{:S(2)}) copy-start(bf16[2,768,384]{2,1,0:T(8,128)(2,1)} %constant.13.clone.row_hbm) | copy-start | bytes 3538948
  1.9 1.1 %copy-start.1 = (bf16[2,768,256]{2,1,0:T(8,128)(2,1)S(1)}, bf16[2,768,256]{2,1,0:T(8,128)(2,1)}, u32[]{:S(2)}) copy-start(bf16[2,768,256]{2,1,0:T(8,128)(2,1)} %constant.14.clone.row_k_hbm) | copy-start | bytes 2359300
  3.0 1.1 %copy-start.2 = (bf16[2,512,384]{2,1,0:T(8,128)(2,1)S(1)}, bf16[2,512,384]{2,1,0:T(8,128)(2,1)}, u32[]{:S(2)}) copy-start(bf16[2,512,384]{2,1,0:T(8,128)(2,1)} %constant.11.clone.back_hbm) | copy-start | bytes 2359300
  4.2 1.1 %copy-start.3 = (bf16[2,384,512]{2,1,0:T(8,128)(2,1)S(1)}, bf16[2,384,512]{2,1,0:T(8,128)(2,1)}, u32[]{:S(2)}) copy-start(bf16[2,384,512]{2,1,0:T(8,128)(2,1)} %constant.10.clone.col_hbm) | copy-start | bytes 2359300
  5.3 1.0 %copy-start.4 = (bf16[2,256,512]{2,1,0:T(8,128)(2,1)S(1)}, bf16[2,256,512]{2,1,0:T(8,128)(2,1)}, u32[]{:S(2)}) copy-start(bf16[2,256,512]{2,1,0:T(8,128)(2,1)} %constant.12.clone.col_k_hbm) | copy-start | bytes 1572868
  6.3 1.0 %copy-start.5 = (f32[2,255,255]{2,0,1:T(2,128)S(1)}, f32[2,255,255]{2,0,1:T(2,128)}, u32[]{:S(2)}) copy-start(f32[2,255,255]{2,0,1:T(2,128)} %param.9) | copy-start | bytes 1560604
  7.4 1.0 %copy-start.6 = (f32[2,128,384]{2,1,0:T(8,128)S(1)}, f32[2,128,384]{2,1,0:T(8,128)}, u32[]{:S(2)}) copy-start(f32[2,128,384]{2,1,0:T(8,128)} %volume_hbm.1) | copy-start | bytes 1179652
  8.4 0.9 %copy-start.7 = (f32[128,384]{1,0:T(8,128)S(1)}, f32[128,384]{1,0:T(8,128)}, u32[]{:S(2)}) copy-start(f32[128,384]{1,0:T(8,128)} %measured_hbm.1) | copy-start | bytes 589828

commit v2 on v1

--- a/solution.py
+++ b/solution.py
@@ -26,20 +26,20 @@
 
 def tables(rows, width, size):
     freq_rows, freq_cols = 3 * rows, width + 128
-    half = freq_cols // 2
     reach = (size - 1) // 2
-    omega = math.pi * (2 * np.arange(half) + 1) / freq_cols
+    omega = math.pi * (2 * np.arange(freq_cols // 2) + 1) / freq_cols
     across = np.arange(width)[:, None] * omega[None, :]
     col = np.concatenate([np.cos(across), -np.sin(across)], 1)
     back = col.T * (2.0 / (freq_cols * freq_rows))
     across_k = (np.arange(size + 1) - reach)[:, None] * omega[None, :]
     col_k = np.concatenate([np.cos(across_k), -np.sin(across_k)], 1)
-    u = np.arange(freq_rows)
-    down = 2 * math.pi / freq_rows * (u[:, None] * u[None, :] % freq_rows)
+    theta = math.pi * (2 * np.arange(freq_rows // 2) + 1) / freq_rows
+    place = np.concatenate([np.arange(2 * rows), np.arange(-rows, 0)])
+    down = theta[:, None] * place[None, :]
     row = np.concatenate([np.cos(down), np.sin(down)], 0)
-    down_k = 2 * math.pi / freq_rows * (u[:, None] * (np.arange(size + 1) - reach)[None, :] % freq_rows)
+    down_k = theta[:, None] * (np.arange(size + 1) - reach)[None, :]
     row_k = np.concatenate([np.cos(down_k), np.sin(down_k)], 0)
-    return [halves(t) for t in (col, back, col_k, row, row_k)]
+    return [halves(t) for t in (col, back, col_k, row, row.T, row_k)]
 
 
 def split(x):
@@ -53,11 +53,21 @@
     return jnp.dot(left, right, preferred_element_type=f32)
 
 
-def turned(a, sign):
+def spectrum(a):
     m, n = a.shape[0] // 2, a.shape[1] // 2
-    real = a[:m, :n] + sign * a[m:, n:]
-    imaginary = a[:m, n:] - sign * a[m:, :n]
-    return real, imaginary
+    cos_real, cos_imaginary, sin_real, sin_imaginary = a[:m, :n], a[:m, n:], a[m:, :n], a[m:, n:]
+    return (
+        cos_real + sin_imaginary,
+        cos_imaginary - sin_real,
+        cos_real - sin_imaginary,
+        cos_imaginary + sin_real,
+    )
+
+
+def folded(plus_real, plus_imaginary, minus_real, minus_imaginary):
+    even = jnp.concatenate([plus_real + minus_real, plus_imaginary + minus_imaginary], axis=1)
+    odd = jnp.concatenate([minus_imaginary - plus_imaginary, plus_real - minus_real], axis=1)
+    return jnp.concatenate([even, odd], axis=0)
 
 
 def kernel(
@@ -71,6 +81,7 @@
     back_hbm,
     col_k_hbm,
     row_hbm,
+    row_back_hbm,
     row_k_hbm,
     next_ref,
     residual_ref,
@@ -81,15 +92,17 @@
     back_ref,
     col_k_ref,
     row_ref,
+    row_back_ref,
     row_k_ref,
     pad_ref,
     optic_ref,
-    mid_ref,
+    sum_ref,
     part_ref,
     pair_ref,
     held_ref,
     beside_ref,
     own_ref,
+    block_ref,
     piece_ref,
     full_ref,
     load_sems,
@@ -99,7 +112,6 @@
     final_sems,
     half_sems,
     halo_sems,
-    relay_sems,
 ):
     depth, tile = lax.axis_index("depth"), lax.axis_index("tile")
     chip, core = depth // 2, depth % 2
@@ -114,10 +126,8 @@
     half_rows = rows // 2
     length = half_rows // chips
     freq_rows, freq_cols = 3 * rows, width + 128
-    half = freq_cols // 2
-
     loads = {}
-    order = ("spread", "col_k", "volume", "col", "row_k", "row", "back", "measured")
+    order = ("spread", "col_k", "volume", "col", "row_k", "row", "row_back", "back", "measured")
     refs = {
         "spread": (spread_hbm, spread_ref),
         "col_k": (col_k_hbm, col_k_ref),
@@ -125,15 +135,18 @@
         "col": (col_hbm, col_ref),
         "row_k": (row_k_hbm, row_k_ref),
         "row": (row_hbm, row_ref),
+        "row_back": (row_back_hbm, row_back_ref),
         "back": (back_hbm, back_ref),
         "measured": (measured_hbm, measured_ref),
     }
     for i, name in enumerate(order):
         loads[name] = pltpu.make_async_copy(*refs[name], load_sems.at[i])
+    for name in order[:4]:
         loads[name].start()
 
     barrier = pltpu.get_barrier_semaphore()
-    peers = [(partner, tile), (depth, above), (depth, below)] + [(t * 2 + core, tile) for t in targets[1:]]
+    peers = [(partner, tile)] + [(d, t) for t in (above, below) for d in (depth, partner)]
+    peers += [(t * 2 + core, tile) for t in targets[1:]]
     for d, t in peers:
         pl.semaphore_signal(barrier, inc=1, device_id=(d, t), device_id_type=MESH)
 
@@ -161,45 +174,44 @@
         pad_ref[d, 0:size, 0:size] = spread_ref[:, d, :]
     stacked = pad_ref[...].reshape(planes * (size + 1), size + 1)
     loads["col_k"].wait()
+    for name in order[4:6]:
+        loads[name].start()
     optic_cols = product(split(stacked), pair(col_k_ref))
     loads["volume"].wait()
     loads["col"].wait()
+    for name in order[6:]:
+        loads[name].start()
     plane_cols = product(split(volume_ref[...].reshape(planes * rows, width)), pair(col_ref))
     loads["row_k"].wait()
     for d in range(planes):
         optic = split(optic_cols[d * (size + 1) : (d + 1) * (size + 1)])
-        real, imaginary = turned(product(pair(row_k_ref), optic), 1.0)
-        optic_ref[d, 0], optic_ref[d, 1] = real, imaginary
+        for k, value in enumerate(spectrum(product(pair(row_k_ref), optic))):
+            optic_ref[d, k] = value
     loads["row"].wait()
     for d in range(planes):
         plane = split(plane_cols[d * rows : (d + 1) * rows])
-        row_part = pair(row_ref, slice(None), slice(0, rows))
-        real, imaginary = turned(product(row_part, plane), 1.0)
-        optic_real, optic_imaginary = optic_ref[d, 0], optic_ref[d, 1]
-        sum_real = optic_real * real - optic_imaginary * imaginary
-        sum_imaginary = optic_real * imaginary + optic_imaginary * real
-        if d == 0:
-            mid_ref[0], mid_ref[1] = sum_real, sum_imaginary
-        else:
-            mid_ref[0] += sum_real
-            mid_ref[1] += sum_imaginary
-    total = split(jnp.concatenate([mid_ref[0], mid_ref[1]], axis=1))
+        values = spectrum(product(pair(row_ref, slice(None), slice(0, rows)), plane))
+        for k in (0, 2):
+            optic_real, optic_imaginary = optic_ref[d, k], optic_ref[d, k + 1]
+            real, imaginary = values[k], values[k + 1]
+            sum_real = optic_real * real - optic_imaginary * imaginary
+            sum_imaginary = optic_real * imaginary + optic_imaginary * real
+            if d == 0:
+                sum_ref[k], sum_ref[k + 1] = sum_real, sum_imaginary
+            else:
+                sum_ref[k] += sum_real
+                sum_ref[k + 1] += sum_imaginary
+    total = split(folded(*(sum_ref[k] for k in range(4))))
 
     def strips_of(first, count):
-        ends = [
-            jnp.concatenate(
-                [row_ref[p, k * freq_rows + first * rows : k * freq_rows + (first + count) * rows] for k in range(2)], axis=0
-            )
-            for p in range(2)
-        ]
-        real, imaginary = turned(product(ends, total), -1.0)
-        mixed = jnp.concatenate([real, imaginary], axis=1)
-        part = product(split(mixed), pair(back_ref))
+        part_rows = pair(row_back_ref, slice(first * rows, (first + count) * rows))
+        part = product(split(product(part_rows, total)), pair(back_ref))
         part_ref[first : first + count] = part.reshape(count, 2, half_rows, width)
 
     def to_partner(b):
         return remote(part_ref.at[b, 1 - core], pair_ref.at[b], pair_sems, (b,), partner, tile)
 
+    loads["row_back"].wait()
     loads["back"].wait()
     strips_of(1, 2)
     pl.semaphore_wait(barrier, len(peers))
@@ -235,7 +247,7 @@
         value += piece_ref[i]
     full_ref[0, core, chip] = value
 
-    finals, halos, halved, relayed = {}, {}, {}, {}
+    finals, halos, halved = {}, {}, {}
     mine = full_ref.at[0, core, chip]
     for i in reversed(range(1, chips)):
         finals[i] = remote(mine, mine, final_sems, (i,), targets[i] * 2 + core, tile)
@@ -244,39 +256,38 @@
         here = full_ref.at[0, core, j]
         if i:
             finals[i].wait_recv()
-        halos[0, i] = remote(here, full_ref.at[2, core, j], halo_sems, (0, i), depth, above)
-        halos[1, i] = remote(here, full_ref.at[1, core, j], halo_sems, (1, i), depth, below)
         halved[i] = remote(here, here, half_sems, (i,), partner, tile)
-    for i in range(chips):
-        for b, block in ((0, 2), (1, 1)):
-            halos[b, i].wait_recv()
-            there = full_ref.at[block, core, sources[i]]
-            relayed[b, i] = remote(there, there, relay_sems, (b, i), partner, tile)
+        for c, d in ((0, depth), (1, partner)):
+            halos[0, c, i] = remote(here, full_ref.at[2, core, j], halo_sems, (0, c, i), d, above)
+            halos[1, c, i] = remote(here, full_ref.at[1, core, j], halo_sems, (1, c, i), d, below)
     for i in range(chips):
         halved[i].wait_recv()
+
     strip = full_ref[0].reshape(rows, width)
     residual_ref[...] = strip
+    strip_cols = split(product(split(strip), pair(col_ref)))
+    block_ref[...] = product(pair(row_ref, slice(None), slice(0, rows)), strip_cols)
     for i in range(chips):
         for b in (0, 1):
-            relayed[b, i].wait_recv()
+            for c in (0, 1):
+                halos[b, c, i].wait_recv()
     after = jnp.where(tile < strips - 1, full_ref[1].reshape(rows, width), 0.0)
     before = jnp.where(tile > 0, full_ref[2].reshape(rows, width), 0.0)
-    block = jnp.concatenate([strip, after, before], axis=0)
-    block_cols = product(split(block), pair(col_ref))
-    real, imaginary = turned(product(pair(row_ref), split(block_cols)), 1.0)
-    mid_ref[0], mid_ref[1] = real, imaginary
+    beside_cols = split(product(split(jnp.concatenate([after, before], axis=0)), pair(col_ref)))
+    block_ref[...] += product(pair(row_ref, slice(None), slice(rows, freq_rows)), beside_cols)
+    mixed = []
     for d in range(planes):
-        real, imaginary = mid_ref[0], mid_ref[1]
-        optic_real, optic_imaginary = optic_ref[d, 0], optic_ref[d, 1]
-        grad_real = optic_real * real + optic_imaginary * imaginary
-        grad_imaginary = optic_real * imaginary - optic_imaginary * real
-        grad = split(jnp.concatenate([grad_real, grad_imaginary], axis=1))
-        ends = [jnp.concatenate([row_ref[p, 0:rows], row_ref[p, freq_rows : freq_rows + rows]], axis=0) for p in range(2)]
-        real, imaginary = turned(product(ends, grad), -1.0)
-        mixed = split(jnp.concatenate([real, imaginary], axis=1))
-        gradient = product(mixed, pair(back_ref))
-        shifted = volume_ref[d] - step_size * gradient
-        next_ref[d] = shifted - jnp.clip(shifted, -threshold, threshold)
+        values = spectrum(block_ref[...])
+        grad = []
+        for k in (0, 2):
+            optic_real, optic_imaginary = optic_ref[d, k], optic_ref[d, k + 1]
+            real, imaginary = values[k], values[k + 1]
+            grad.append(optic_real * real + optic_imaginary * imaginary)
+            grad.append(optic_real * imaginary - optic_imaginary * real)
+        mixed.append(product(pair(row_back_ref, slice(0, rows)), split(folded(*grad))))
+    gradient = product(split(jnp.concatenate(mixed, axis=0)), pair(back_ref)).reshape(planes, rows, width)
+    shifted = volume_ref[...] - step_size * gradient
+    next_ref[...] = shifted - jnp.clip(shifted, -threshold, threshold)
     for copy in sends:
         copy.wait_send()
 
@@ -299,36 +310,36 @@
     freq_rows, half = 3 * rows, (width + 128) // 2
     vmem = pl.BlockSpec(memory_space=pltpu.VMEM)
     dma = pltpu.SemaphoreType.DMA
-    inputs = (volume, spread, measured, *constants)
+    inputs = tuple(pltpu.with_memory_space_constraint(a, pltpu.HBM) for a in (volume, spread, measured, *constants))
     shapes = (jax.ShapeDtypeStruct((planes, rows, width), f32), jax.ShapeDtypeStruct((rows, width), f32))
     outs = pl.pallas_call(
         functools.partial(kernel, steps, nx, strips),
         out_shape=shapes,
-        in_specs=[pl.BlockSpec(memory_space=pltpu.HBM)] * 8,
+        in_specs=[pl.BlockSpec(memory_space=pl.ANY)] * 9,
         out_specs=(vmem, vmem),
         scratch_shapes=[pltpu.VMEM(a.shape, a.dtype) for a in inputs]
         + [
             pltpu.VMEM((planes, size + 1, size + 1), f32),
-            pltpu.VMEM((planes, 2, freq_rows, half), f32),
-            pltpu.VMEM((2, freq_rows, half), f32),
+            pltpu.VMEM((planes, 4, freq_rows // 2, half), f32),
+            pltpu.VMEM((4, freq_rows // 2, half), f32),
             pltpu.VMEM((3, 2, half_rows, width), f32),
             pltpu.VMEM((3, half_rows, width), f32),
             pltpu.VMEM((3, chips, length, width), f32),
             pltpu.VMEM((2, chips, length, width), f32),
             pltpu.VMEM((chips, length, width), f32),
+            pltpu.VMEM((freq_rows, 2 * half), f32),
             pltpu.VMEM((chips, length, width), f32),
             pltpu.VMEM((3, 2, chips, length, width), f32),
-            dma((8,)),
+            dma((9,)),
             dma((2, 3)),
             dma((2, 2, chips)),
             dma((2, chips)),
             dma((2, chips)),
             dma((2, chips)),
-            dma((2, 2, chips)),
-            dma((2, 2, chips)),
+            dma((2, 2, 2, chips)),
         ],
         compiler_params=pltpu.CompilerParams(
-            collective_id=0, has_side_effects=True, vmem_limit_bytes=24 * 2**20
+            collective_id=0, has_side_effects=True, vmem_limit_bytes=20 * 2**20
         ),
     )(*inputs)
     return pl.pallas_call(

time: 49 us -> 34.9 us (0.71)
  local copies, waits for them, and re-layouts: 8.67 us -> 0 us
  Pallas kernels: 39.2 us -> 34.1 us
    unnamed x16 -> x0, local copies, waits for them, and re-layouts: 8.67 us -> none
    pallas_call x1, Pallas kernels: 38.4 us -> 33.2 us  [per_device(): pl.pallas_call(functools.partial(kernel, steps, nx, strips), out_shape=sh...]
where the time goes in v2:
time: 34.9 us; the launch traced here: 34.7 us
  Pallas kernels  34.1 us (98%)
  between operations  0.64 us (2%)
    pallas_call x1, Pallas kernels, per_device(): pl.pallas_call(functools.partial(kernel, steps, nx, strips), out_shape=sh...  33.2 us
    pallas_call x1, Pallas kernels, per_device(): pl.pallas_call(finish, out_shape=shapes, in_specs=[vmem, vmem], out_specs...  0.85 us

profile of v2, /device:TPU:1, one launch (start us, length us, event | category | flops | bytes accessed | tf_op | source)
XLA Modules:
  0.0 34.7 jit_solution(6072433260819841202)
XLA Ops:
  0.6 33.2 %shard_map.104 = (f32[2,128,384]{2,1,0:T(8,128)S(1)}, f32[128,384]{1,0:T(8,128)S(1)}) custom-call(f32[2,128,384]{2,1,0:T(8,128)} %volume_hbm.1, f32[255,2,255]{2,1,0:T(2,128)} %bitcast.1, f32[128,384]{1,0:T(8,128)} %measured_hbm.1, bf16[2,384,512]{2,1,0:T(8,128)(2,1)} %constant.12.clone.col_hbm, bf16[2,512,384]{2,1,0:T(8,128)(2,1)} %constant.13.clone.back_hbm, ...), custom_call_target="tpu_custom_call" | custom-call | tf_op jit(solution)/shard_map/pallas_call | solution.py:315
  33.9 0.8 %shard_map.105 = (f32[2,128,384]{2,1,0:T(8,128)}, f32[128,384]{1,0:T(8,128)}) custom-call(f32[2,128,384]{2,1,0:T(8,128)S(1)} %get-tuple-element.4.next_ref, f32[128,384]{1,0:T(8,128)S(1)} %get-tuple-element.5.residual_ref), custom_call_target="tpu_custom_call" | custom-call | tf_op jit(solution)/shard_map/pallas_call | solution.py:345

commit v3 on v2

--- a/solution.py
+++ b/solution.py
@@ -68,6 +68,13 @@
     even = jnp.concatenate([plus_real + minus_real, plus_imaginary + minus_imaginary], axis=1)
     odd = jnp.concatenate([minus_imaginary - plus_imaginary, plus_real - minus_real], axis=1)
     return jnp.concatenate([even, odd], axis=0)
+
+
+def when(condition, action):
+    if condition is None:
+        action()
+    else:
+        pl.when(condition)(action)
 
 
 def kernel(
@@ -118,7 +125,11 @@
     x, y = chip // 2, chip % 2
     partner = chip * 2 + (1 - core)
     above, below = (tile + 1) % strips, (tile + strips - 1) % strips
+    has_above, has_below = tile < strips - 1, tile > 0
     chips = len(steps)
+    hops = [min(dx, nx - dx) + 2 * dy for dx, dy in steps]
+    far = [i for i in range(chips) if hops[i] >= 2]
+    far_out = [i for i in range(chips) if hops[i] >= 1]
     targets = [(x + dx) % nx * 2 + (y + dy) % 2 for dx, dy in steps]
     sources = [(x + nx - dx) % nx * 2 + (y + dy) % 2 for dx, dy in steps]
     planes, rows, width = volume_ref.shape
@@ -141,18 +152,25 @@
     }
     for i, name in enumerate(order):
         loads[name] = pltpu.make_async_copy(*refs[name], load_sems.at[i])
-    for name in order[:4]:
+    for name in order:
         loads[name].start()
 
     barrier = pltpu.get_barrier_semaphore()
-    peers = [(partner, tile)] + [(d, t) for t in (above, below) for d in (depth, partner)]
-    peers += [(t * 2 + core, tile) for t in targets[1:]]
-    for d, t in peers:
-        pl.semaphore_signal(barrier, inc=1, device_id=(d, t), device_id_type=MESH)
+    inside = [partner] + [t * 2 + core for t in targets[1:]]
+    across = [depth, partner] + [targets[i] * 2 + core for i in sorted({*far, *far_out})]
+
+    def greet(devices, t):
+        for d in devices:
+            pl.semaphore_signal(barrier, inc=1, device_id=(d, t), device_id_type=MESH)
+
+    greet(inside, tile)
+    when(has_above, lambda: greet(across, above))
+    when(has_below, lambda: greet(across, below))
+    arrivals = len(inside) + sum(jnp.where(side, len(across), 0) for side in (has_above, has_below))
 
     sends = []
 
-    def remote(src, dst, sems, index, d, t):
+    def remote(src, dst, sems, index, d, t, going=None, coming=None):
         copy = pltpu.make_async_remote_copy(
             src_ref=src,
             dst_ref=dst,
@@ -161,9 +179,11 @@
             device_id=(d, t),
             device_id_type=MESH,
         )
-        copy.start()
-        sends.append(copy)
-        return copy
+        when(going, copy.start)
+        sends.append(lambda: when(going, copy.wait_send))
+        return lambda: when(coming, copy.wait_recv)
+
+    sides = ((above, has_above, has_below), (below, has_below, has_above))
 
     def pair(ref, *index):
         return ref[(0, *index)], ref[(1, *index)]
@@ -172,35 +192,37 @@
     loads["spread"].wait()
     for d in range(planes):
         pad_ref[d, 0:size, 0:size] = spread_ref[:, d, :]
+    loads["col_k"].wait()
     stacked = pad_ref[...].reshape(planes * (size + 1), size + 1)
-    loads["col_k"].wait()
-    for name in order[4:6]:
-        loads[name].start()
     optic_cols = product(split(stacked), pair(col_k_ref))
     loads["volume"].wait()
     loads["col"].wait()
-    for name in order[6:]:
-        loads[name].start()
+    loads["row_k"].wait()
+    loads["row"].wait()
+    optic = split(optic_cols[0 * (size + 1) : (0 + 1) * (size + 1)])
+    for k, value in enumerate(spectrum(product(pair(row_k_ref), optic))):
+        optic_ref[0, k] = value
     plane_cols = product(split(volume_ref[...].reshape(planes * rows, width)), pair(col_ref))
-    loads["row_k"].wait()
-    for d in range(planes):
-        optic = split(optic_cols[d * (size + 1) : (d + 1) * (size + 1)])
-        for k, value in enumerate(spectrum(product(pair(row_k_ref), optic))):
-            optic_ref[d, k] = value
-    loads["row"].wait()
-    for d in range(planes):
-        plane = split(plane_cols[d * rows : (d + 1) * rows])
-        values = spectrum(product(pair(row_ref, slice(None), slice(0, rows)), plane))
-        for k in (0, 2):
-            optic_real, optic_imaginary = optic_ref[d, k], optic_ref[d, k + 1]
-            real, imaginary = values[k], values[k + 1]
-            sum_real = optic_real * real - optic_imaginary * imaginary
-            sum_imaginary = optic_real * imaginary + optic_imaginary * real
-            if d == 0:
-                sum_ref[k], sum_ref[k + 1] = sum_real, sum_imaginary
-            else:
-                sum_ref[k] += sum_real
-                sum_ref[k + 1] += sum_imaginary
+    plane = split(plane_cols[0 * rows : (0 + 1) * rows])
+    values = spectrum(product(pair(row_ref, slice(None), slice(0, rows)), plane))
+    for k in (0, 2):
+        optic_real, optic_imaginary = optic_ref[0, k], optic_ref[0, k + 1]
+        real, imaginary = values[k], values[k + 1]
+        sum_real = optic_real * real - optic_imaginary * imaginary
+        sum_imaginary = optic_real * imaginary + optic_imaginary * real
+        sum_ref[k], sum_ref[k + 1] = sum_real, sum_imaginary
+    optic = split(optic_cols[1 * (size + 1) : (1 + 1) * (size + 1)])
+    for k, value in enumerate(spectrum(product(pair(row_k_ref), optic))):
+        optic_ref[1, k] = value
+    plane = split(plane_cols[1 * rows : (1 + 1) * rows])
+    values = spectrum(product(pair(row_ref, slice(None), slice(0, rows)), plane))
+    for k in (0, 2):
+        optic_real, optic_imaginary = optic_ref[1, k], optic_ref[1, k + 1]
+        real, imaginary = values[k], values[k + 1]
+        sum_real = optic_real * real - optic_imaginary * imaginary
+        sum_imaginary = optic_real * imaginary + optic_imaginary * real
+        sum_ref[k] += sum_real
+        sum_ref[k + 1] += sum_imaginary
     total = split(folded(*(sum_ref[k] for k in range(4))))
 
     def strips_of(first, count):
@@ -214,28 +236,36 @@
     loads["row_back"].wait()
     loads["back"].wait()
     strips_of(1, 2)
-    pl.semaphore_wait(barrier, len(peers))
+    pl.semaphore_wait(barrier, arrivals)
     paired = {b: to_partner(b) for b in (1, 2)}
     strips_of(0, 1)
     paired[0] = to_partner(0)
 
     near = {}
     for b in (1, 2):
-        paired[b].wait_recv()
+        paired[b]()
         held_ref[b - 1] = (part_ref[b, core] + pair_ref[b]).reshape(chips, length, width)
     for i in reversed(range(chips)):
-        for b, t in ((0, above), (1, below)):
-            near[b, i] = remote(held_ref.at[b, targets[i]], beside_ref.at[b, i], tile_sems, (b, i), depth, t)
-    paired[0].wait_recv()
+        for b, side in enumerate(sides):
+            to = targets[i] * 2 + core if i in far else depth
+            near[b, i] = remote(held_ref.at[b, targets[i]], beside_ref.at[b, i], tile_sems, (b, i), to, *side)
+    paired[0]()
     own_ref[...] = (part_ref[0, core] + pair_ref[0]).reshape(chips, length, width)
 
     pieces = {}
+
+    def from_beside(i):
+        near[0, i]()
+        near[1, i]()
+        value = jnp.where(has_below, beside_ref[0, i], 0.0)
+        return value + jnp.where(has_above, beside_ref[1, i], 0.0)
+
+    for i in far:
+        pieces[i] = remote(own_ref.at[targets[i]], piece_ref.at[i], piece_sems, (i,), targets[i] * 2 + core, tile)
     for i in reversed(range(chips)):
-        near[0, i].wait_recv()
-        near[1, i].wait_recv()
-        value = own_ref[targets[i]]
-        value += jnp.where(tile > 0, beside_ref[0, i], 0.0)
-        value += jnp.where(tile < strips - 1, beside_ref[1, i], 0.0)
+        if i in far:
+            continue
+        value = own_ref[targets[i]] + from_beside(i)
         if i:
             held_ref[2, i] = value
             pieces[i] = remote(held_ref.at[2, i], piece_ref.at[i], piece_sems, (i,), targets[i] * 2 + core, tile)
@@ -243,25 +273,37 @@
     start = pl.multiple_of(core * half_rows + chip * length, length)
     value -= measured_ref[pl.ds(start, length), :]
     for i in range(1, chips):
-        pieces[i].wait_recv()
+        pieces[i]()
         value += piece_ref[i]
+        if i in far:
+            value += from_beside(i)
     full_ref[0, core, chip] = value
 
     finals, halos, halved = {}, {}, {}
     mine = full_ref.at[0, core, chip]
     for i in reversed(range(1, chips)):
-        finals[i] = remote(mine, mine, final_sems, (i,), targets[i] * 2 + core, tile)
+        to = targets[i] * 2 + core
+        finals[i] = remote(mine, mine, final_sems, (i,), to, tile)
+        if i in far_out:
+            for b, side in enumerate(sides):
+                halos[b, 0, i] = remote(mine, full_ref.at[2 - b, core, chip], halo_sems, (b, 0, i), to, *side)
     for i in range(chips):
         j = sources[i]
         here = full_ref.at[0, core, j]
         if i:
-            finals[i].wait_recv()
+            finals[i]()
         halved[i] = remote(here, here, half_sems, (i,), partner, tile)
-        for c, d in ((0, depth), (1, partner)):
-            halos[0, c, i] = remote(here, full_ref.at[2, core, j], halo_sems, (0, c, i), d, above)
-            halos[1, c, i] = remote(here, full_ref.at[1, core, j], halo_sems, (1, c, i), d, below)
+        if i not in far_out:
+            for b, side in enumerate(sides):
+                for c, d in enumerate((depth, partner)):
+                    halos[b, c, i] = remote(here, full_ref.at[2 - b, core, j], halo_sems, (b, c, i), d, *side)
+    for i in far_out:
+        for b, (_, _, coming) in enumerate(sides):
+            halos[b, 0, i]()
+            there = full_ref.at[2 - b, core, sources[i]]
+            halos[b, 1, i] = remote(there, there, halo_sems, (b, 1, i), partner, tile, coming, coming)
     for i in range(chips):
-        halved[i].wait_recv()
+        halved[i]()
 
     strip = full_ref[0].reshape(rows, width)
     residual_ref[...] = strip
@@ -269,10 +311,10 @@
     block_ref[...] = product(pair(row_ref, slice(None), slice(0, rows)), strip_cols)
     for i in range(chips):
         for b in (0, 1):
-            for c in (0, 1):
-                halos[b, c, i].wait_recv()
-    after = jnp.where(tile < strips - 1, full_ref[1].reshape(rows, width), 0.0)
-    before = jnp.where(tile > 0, full_ref[2].reshape(rows, width), 0.0)
+            for c in (1,) if i in far_out else (0, 1):
+                halos[b, c, i]()
+    after = jnp.where(has_above, full_ref[1].reshape(rows, width), 0.0)
+    before = jnp.where(has_below, full_ref[2].reshape(rows, width), 0.0)
     beside_cols = split(product(split(jnp.concatenate([after, before], axis=0)), pair(col_ref)))
     block_ref[...] += product(pair(row_ref, slice(None), slice(rows, freq_rows)), beside_cols)
     mixed = []
@@ -288,8 +330,8 @@
     gradient = product(split(jnp.concatenate(mixed, axis=0)), pair(back_ref)).reshape(planes, rows, width)
     shifted = volume_ref[...] - step_size * gradient
     next_ref[...] = shifted - jnp.clip(shifted, -threshold, threshold)
-    for copy in sends:
-        copy.wait_send()
+    for wait in sends:
+        wait()
 
 
 def finish(next_ref, residual_ref, next_out, residual_out):

time: 34.9 us -> 31.6 us (0.905)
  the two profiles are of different devices: /device:TPU:1 before, /device:TPU:9 now
where the time goes in v3:
time: 31.6 us; the launch traced here: 31.5 us
  Pallas kernels  30.9 us (98%)
  between operations  0.64 us (2%)
    pallas_call x1, Pallas kernels, per_device(): pl.pallas_call(functools.partial(kernel, steps, nx, strips), out_shape=sh...  30 us
    pallas_call x1, Pallas kernels, per_device(): pl.pallas_call(finish, out_shape=shapes, in_specs=[vmem, vmem], out_specs...  0.85 us

profile of v3, /device:TPU:9, one launch (start us, length us, event | category | flops | bytes accessed | tf_op | source)
XLA Modules:
  0.0 31.5 jit_solution(353459118435071838)
XLA Ops:
  0.6 30.0 %shard_map.104 = (f32[2,128,384]{2,1,0:T(8,128)S(1)}, f32[128,384]{1,0:T(8,128)S(1)}) custom-call(f32[2,128,384]{2,1,0:T(8,128)} %volume_hbm.1, f32[255,2,255]{2,1,0:T(2,128)} %bitcast.1, f32[128,384]{1,0:T(8,128)} %measured_hbm.1, bf16[2,384,512]{2,1,0:T(8,128)(2,1)} %constant.12.clone.col_hbm, bf16[2,512,384]{2,1,0:T(8,128)(2,1)} %constant.13.clone.back_hbm, ...), custom_call_target="tpu_custom_call" | custom-call | tf_op jit(solution)/shard_map/pallas_call | solution.py:357
  30.7 0.8 %shard_map.105 = (f32[2,128,384]{2,1,0:T(8,128)}, f32[128,384]{1,0:T(8,128)}) custom-call(f32[2,128,384]{2,1,0:T(8,128)S(1)} %get-tuple-element.4.next_ref, f32[128,384]{1,0:T(8,128)S(1)} %get-tuple-element.5.residual_ref), custom_call_target="tpu_custom_call" | custom-call | tf_op jit(solution)/shard_map/pallas_call | solution.py:387

commit v4 on v3

--- a/solution.py
+++ b/solution.py
@@ -105,6 +105,7 @@
     optic_ref,
     sum_ref,
     part_ref,
+    kept_ref,
     pair_ref,
     held_ref,
     beside_ref,
@@ -128,7 +129,7 @@
     has_above, has_below = tile < strips - 1, tile > 0
     chips = len(steps)
     hops = [min(dx, nx - dx) + 2 * dy for dx, dy in steps]
-    far = [i for i in range(chips) if hops[i] >= 2]
+    far = [i for i in range(chips) if hops[i] >= 1]
     far_out = [i for i in range(chips) if hops[i] >= 1]
     targets = [(x + dx) % nx * 2 + (y + dy) % 2 for dx, dy in steps]
     sources = [(x + nx - dx) % nx * 2 + (y + dy) % 2 for dx, dy in steps]
@@ -225,32 +226,29 @@
         sum_ref[k + 1] += sum_imaginary
     total = split(folded(*(sum_ref[k] for k in range(4))))
 
-    def strips_of(first, count):
-        part_rows = pair(row_back_ref, slice(first * rows, (first + count) * rows))
+    def half_of(c):
+        first = [pl.multiple_of(b * rows + c * half_rows, half_rows) for b in range(3)]
+        part_rows = [jnp.concatenate([row_back_ref[p, pl.ds(f, half_rows), :] for f in first], axis=0) for p in range(2)]
         part = product(split(product(part_rows, total)), pair(back_ref))
-        part_ref[first : first + count] = part.reshape(count, 2, half_rows, width)
-
-    def to_partner(b):
-        return remote(part_ref.at[b, 1 - core], pair_ref.at[b], pair_sems, (b,), partner, tile)
+        return part.reshape(3, half_rows, width)
 
     loads["row_back"].wait()
     loads["back"].wait()
-    strips_of(1, 2)
+    part_ref[...] = half_of(1 - core)
     pl.semaphore_wait(barrier, arrivals)
-    paired = {b: to_partner(b) for b in (1, 2)}
-    strips_of(0, 1)
-    paired[0] = to_partner(0)
+    paired = {b: remote(part_ref.at[b], pair_ref.at[b], pair_sems, (b,), partner, tile) for b in (1, 2, 0)}
+    kept_ref[...] = half_of(core)
 
     near = {}
     for b in (1, 2):
         paired[b]()
-        held_ref[b - 1] = (part_ref[b, core] + pair_ref[b]).reshape(chips, length, width)
+        held_ref[b - 1] = (kept_ref[b] + pair_ref[b]).reshape(chips, length, width)
     for i in reversed(range(chips)):
         for b, side in enumerate(sides):
             to = targets[i] * 2 + core if i in far else depth
             near[b, i] = remote(held_ref.at[b, targets[i]], beside_ref.at[b, i], tile_sems, (b, i), to, *side)
     paired[0]()
-    own_ref[...] = (part_ref[0, core] + pair_ref[0]).reshape(chips, length, width)
+    own_ref[...] = (kept_ref[0] + pair_ref[0]).reshape(chips, length, width)
 
     pieces = {}
 
@@ -334,9 +332,15 @@
         wait()
 
 
-def finish(next_ref, residual_ref, next_out, residual_out):
-    next_out[...] = next_ref[...]
-    residual_out[...] = residual_ref[...]
+def finish(next_ref, residual_ref, next_out, residual_out, sems):
+    copies = [
+        pltpu.make_async_copy(next_ref, next_out, sems.at[0]),
+        pltpu.make_async_copy(residual_ref, residual_out, sems.at[1]),
+    ]
+    for copy in copies:
+        copy.start()
+    for copy in copies:
+        copy.wait()
 
 
 def per_device(volume, point_spread, measured):
@@ -364,7 +368,8 @@
             pltpu.VMEM((planes, size + 1, size + 1), f32),
             pltpu.VMEM((planes, 4, freq_rows // 2, half), f32),
             pltpu.VMEM((4, freq_rows // 2, half), f32),
-            pltpu.VMEM((3, 2, half_rows, width), f32),
+            pltpu.VMEM((3, half_rows, width), f32),
+            pltpu.VMEM((3, half_rows, width), f32),
             pltpu.VMEM((3, half_rows, width), f32),
             pltpu.VMEM((3, chips, length, width), f32),
             pltpu.VMEM((2, chips, length, width), f32),
@@ -388,7 +393,8 @@
         finish,
         out_shape=shapes,
         in_specs=[vmem, vmem],
-        out_specs=(vmem, vmem),
+        out_specs=(pl.BlockSpec(memory_space=pl.ANY), pl.BlockSpec(memory_space=pl.ANY)),
+        scratch_shapes=[dma((2,))],
         compiler_params=pltpu.CompilerParams(vmem_limit_bytes=8 * 2**20),
     )(*outs)
 

time: 31.6 us -> 31 us (0.981)
  Pallas kernels: 30.9 us -> 30.3 us
    pallas_call x1, Pallas kernels: 30 us -> 29.5 us  [per_device(): pl.pallas_call(functools.partial(kernel, steps, nx, strips), out_shape=sh...]
where the time goes in v4:
time: 31 us
  Pallas kernels  30.3 us (98%)
  between operations  0.64 us (2%)
    pallas_call x1, Pallas kernels, per_device(): pl.pallas_call(functools.partial(kernel, steps, nx, strips), out_shape=sh...  29.5 us
    pallas_call x1, Pallas kernels, per_device(): pl.pallas_call(finish, out_shape=shapes, in_specs=[vmem, vmem], out_specs...  0.83 us

profile of v4, /device:TPU:9, one launch (start us, length us, event | category | flops | bytes accessed | tf_op | source)
XLA Modules:
  0.0 31.0 jit_solution(11548438249994057420)
XLA Ops:
  0.6 29.5 %shard_map.104 = (f32[2,128,384]{2,1,0:T(8,128)S(1)}, f32[128,384]{1,0:T(8,128)S(1)}) custom-call(f32[2,128,384]{2,1,0:T(8,128)} %volume_hbm.1, f32[255,2,255]{2,1,0:T(2,128)} %bitcast.1, f32[128,384]{1,0:T(8,128)} %measured_hbm.1, bf16[2,384,512]{2,1,0:T(8,128)(2,1)} %constant.12.clone.col_hbm, bf16[2,512,384]{2,1,0:T(8,128)(2,1)} %constant.13.clone.back_hbm, ...), custom_call_target="tpu_custom_call" | custom-call | tf_op jit(solution)/shard_map/pallas_call | solution.py:361
  30.1 0.8 %shard_map.105 = (f32[2,128,384]{2,1,0:T(8,128)}, f32[128,384]{1,0:T(8,128)}) custom-call(f32[2,128,384]{2,1,0:T(8,128)S(1)} %get-tuple-element.4.next_ref, f32[128,384]{1,0:T(8,128)S(1)} %get-tuple-element.5.residual_ref), custom_call_target="tpu_custom_call" | custom-call | tf_op jit(solution)/shard_map/pallas_call | solution.py:392

commit v5 on v4

--- a/solution.py
+++ b/solution.py
@@ -196,40 +196,48 @@
     loads["col_k"].wait()
     stacked = pad_ref[...].reshape(planes * (size + 1), size + 1)
     optic_cols = product(split(stacked), pair(col_k_ref))
-    loads["volume"].wait()
-    loads["col"].wait()
-    loads["row_k"].wait()
-    loads["row"].wait()
-    optic = split(optic_cols[0 * (size + 1) : (0 + 1) * (size + 1)])
-    for k, value in enumerate(spectrum(product(pair(row_k_ref), optic))):
-        optic_ref[0, k] = value
+    for name in ("volume", "col", "row_k", "row"):
+        loads[name].wait()
+    half = freq_cols // 2
+    chunks = [slice(i * half // 2, (i + 1) * half // 2) for i in range(2)]
+
+    def optic_spectrum(d):
+        optic = split(optic_cols[d * (size + 1) : (d + 1) * (size + 1)])
+        for k, value in enumerate(spectrum(product(pair(row_k_ref), optic))):
+            optic_ref[d, k] = value
+
+    def add_plane(d):
+        plane = split(plane_cols[d * rows : (d + 1) * rows])
+        for c in chunks:
+            beyond = slice(half + c.start, half + c.stop)
+            part = [jnp.concatenate([p[:, c], p[:, beyond]], axis=1) for p in plane]
+            values = spectrum(product(pair(row_ref, slice(None), slice(0, rows)), part))
+            for k in (0, 2):
+                optic_real, optic_imaginary = optic_ref[d, k, :, c], optic_ref[d, k + 1, :, c]
+                real, imaginary = values[k], values[k + 1]
+                sum_real = optic_real * real - optic_imaginary * imaginary
+                sum_imaginary = optic_real * imaginary + optic_imaginary * real
+                if d == 0:
+                    sum_ref[k, :, c], sum_ref[k + 1, :, c] = sum_real, sum_imaginary
+                else:
+                    sum_ref[k, :, c] += sum_real
+                    sum_ref[k + 1, :, c] += sum_imaginary
+
+    optic_spectrum(0)
     plane_cols = product(split(volume_ref[...].reshape(planes * rows, width)), pair(col_ref))
-    plane = split(plane_cols[0 * rows : (0 + 1) * rows])
-    values = spectrum(product(pair(row_ref, slice(None), slice(0, rows)), plane))
-    for k in (0, 2):
-        optic_real, optic_imaginary = optic_ref[0, k], optic_ref[0, k + 1]
-        real, imaginary = values[k], values[k + 1]
-        sum_real = optic_real * real - optic_imaginary * imaginary
-        sum_imaginary = optic_real * imaginary + optic_imaginary * real
-        sum_ref[k], sum_ref[k + 1] = sum_real, sum_imaginary
-    optic = split(optic_cols[1 * (size + 1) : (1 + 1) * (size + 1)])
-    for k, value in enumerate(spectrum(product(pair(row_k_ref), optic))):
-        optic_ref[1, k] = value
-    plane = split(plane_cols[1 * rows : (1 + 1) * rows])
-    values = spectrum(product(pair(row_ref, slice(None), slice(0, rows)), plane))
-    for k in (0, 2):
-        optic_real, optic_imaginary = optic_ref[1, k], optic_ref[1, k + 1]
-        real, imaginary = values[k], values[k + 1]
-        sum_real = optic_real * real - optic_imaginary * imaginary
-        sum_imaginary = optic_real * imaginary + optic_imaginary * real
-        sum_ref[k] += sum_real
-        sum_ref[k + 1] += sum_imaginary
-    total = split(folded(*(sum_ref[k] for k in range(4))))
+    for d in range(planes):
+        if d:
+            optic_spectrum(d)
+        add_plane(d)
+    totals = [split(folded(*(sum_ref[k, :, c] for k in range(4)))) for c in chunks]
 
     def half_of(c):
         first = [pl.multiple_of(b * rows + c * half_rows, half_rows) for b in range(3)]
         part_rows = [jnp.concatenate([row_back_ref[p, pl.ds(f, half_rows), :] for f in first], axis=0) for p in range(2)]
-        part = product(split(product(part_rows, total)), pair(back_ref))
+        mixed = [product(part_rows, total) for total in totals]
+        n = mixed[0].shape[1] // 2
+        mixed = jnp.concatenate([m[:, :n] for m in mixed] + [m[:, n:] for m in mixed], axis=1)
+        part = product(split(mixed), pair(back_ref))
         return part.reshape(3, half_rows, width)
 
     loads["row_back"].wait()

time: 31 us -> 31 us (level)
  no operation moved by 1% of the time
where the time goes in v5:
time: 31 us
  Pallas kernels  30.3 us (98%)
  between operations  0.64 us (2%)
    pallas_call x1, Pallas kernels, per_device(): pl.pallas_call(functools.partial(kernel, steps, nx, strips), out_shape=sh...  29.5 us
    pallas_call x1, Pallas kernels, per_device(): pl.pallas_call(finish, out_shape=shapes, in_specs=[vmem, vmem], out_specs...  0.83 us

profile of v5, /device:TPU:9, one launch (start us, length us, event | category | flops | bytes accessed | tf_op | source)
XLA Modules:
  0.0 31.0 jit_solution(9582552004415433532)
XLA Ops:
  0.6 29.5 %shard_map.104 = (f32[2,128,384]{2,1,0:T(8,128)S(1)}, f32[128,384]{1,0:T(8,128)S(1)}) custom-call(f32[2,128,384]{2,1,0:T(8,128)} %volume_hbm.1, f32[255,2,255]{2,1,0:T(2,128)} %bitcast.1, f32[128,384]{1,0:T(8,128)} %measured_hbm.1, bf16[2,384,512]{2,1,0:T(8,128)(2,1)} %constant.12.clone.col_hbm, bf16[2,512,384]{2,1,0:T(8,128)(2,1)} %constant.13.clone.back_hbm, ...), custom_call_target="tpu_custom_call" | custom-call | tf_op jit(solution)/shard_map/pallas_call | solution.py:369
  30.1 0.8 %shard_map.105 = (f32[2,128,384]{2,1,0:T(8,128)}, f32[128,384]{1,0:T(8,128)}) custom-call(f32[2,128,384]{2,1,0:T(8,128)S(1)} %get-tuple-element.4.next_ref, f32[128,384]{1,0:T(8,128)S(1)} %get-tuple-element.5.residual_ref), custom_call_target="tpu_custom_call" | custom-call | tf_op jit(solution)/shard_map/pallas_call | solution.py:400

commit v6 on v4

--- a/solution.py
+++ b/solution.py
@@ -279,7 +279,7 @@
 
     finals, halos, halved = {}, {}, {}
     mine = full_ref.at[0, core, chip]
-    for i in reversed(range(1, chips)):
+    for i in range(1, chips):
         to = targets[i] * 2 + core
         finals[i] = remote(mine, mine, final_sems, (i,), to, tile)
         if i in far_out:

time: 31 us -> 30.6 us (0.987)
  the two profiles are of different devices: /device:TPU:9 before, /device:TPU:1 now
where the time goes in v6:
time: 30.6 us; the launch traced here: 30 us
  Pallas kernels  29.4 us (96%)
  between operations  0.64 us (2%)
    pallas_call x1, Pallas kernels, per_device(): pl.pallas_call(functools.partial(kernel, steps, nx, strips), out_shape=sh...  28.6 us
    pallas_call x1, Pallas kernels, per_device(): pl.pallas_call(finish, out_shape=shapes, in_specs=[vmem, vmem], out_specs...  0.83 us

profile of v6, /device:TPU:1, one launch (start us, length us, event | category | flops | bytes accessed | tf_op | source)
XLA Modules:
  0.0 30.0 jit_solution(3000200707534476788)
XLA Ops:
  0.6 28.6 %shard_map.104 = (f32[2,128,384]{2,1,0:T(8,128)S(1)}, f32[128,384]{1,0:T(8,128)S(1)}) custom-call(f32[2,128,384]{2,1,0:T(8,128)} %volume_hbm.1, f32[255,2,255]{2,1,0:T(2,128)} %bitcast.1, f32[128,384]{1,0:T(8,128)} %measured_hbm.1, bf16[2,384,512]{2,1,0:T(8,128)(2,1)} %constant.12.clone.col_hbm, bf16[2,512,384]{2,1,0:T(8,128)(2,1)} %constant.13.clone.back_hbm, ...), custom_call_target="tpu_custom_call" | custom-call | tf_op jit(solution)/shard_map/pallas_call | solution.py:361
  29.2 0.8 %shard_map.105 = (f32[2,128,384]{2,1,0:T(8,128)}, f32[128,384]{1,0:T(8,128)}) custom-call(f32[2,128,384]{2,1,0:T(8,128)S(1)} %get-tuple-element.4.next_ref, f32[128,384]{1,0:T(8,128)S(1)} %get-tuple-element.5.residual_ref), custom_call_target="tpu_custom_call" | custom-call | tf_op jit(solution)/shard_map/pallas_call | solution.py:392
